TPU v7x, 256 devices: a whole 4x4x8 slice. The times are simulated.
256 devices in a mesh: fsdp: 32 (over z, y_hi, core), dp: 8 (over y_lo, x).
Axes of the slice: x: 4, y: 4 (y_hi: 2, y_lo: 2; y = y_hi * 2 + y_lo), z: 8, core: 2. Of those that a mesh axis runs over, the one named last changes fastest.
Arguments:
- features: bfloat16 [256, 16, 16, 640], P(('fsdp', 'dp')), may hold values from -100 to 100
- weight: bfloat16 [640, 5760], P('fsdp'), may hold values from -0.078125 to 0.078125
- group_norm_gain: float32 [640], replicated, may hold values from 0.1 to 1.9
- group_norm_shift: float32 [640], replicated, may hold values from -3 to 3
- conv_bias: float32 [640], replicated, may hold values from -3 to 3
- cotangent: bfloat16 [256, 16, 16, 640], P(('fsdp', 'dp')), may hold values from -6 to 6
Outputs:
- output: bfloat16 [256, 16, 16, 640], P(('fsdp', 'dp'))
- feature_gradient: bfloat16 [256, 16, 16, 640], P(('fsdp', 'dp'))
- weight_grad: float32 [640, 5760], P('fsdp')
- gain_gradient: float32 [640], replicated
- shift_grad: float32 [640], replicated
- bias_grad: float32 [640], replicated
All inputs are finite; a program needn't handle non-finite values.
Results may differ from a plain program's by a relative error of at most 0.0044.
Values may be sent and summed in bfloat16 or wider, within the bound.
A program may use at most 128 MiB of HBM per device.

v0:
```python
import jax
import jax.numpy as jnp
from jax import lax
from jax.sharding import PartitionSpec as P

GSIZE = 40
epsilon = 1e-05


def group_average(values):
    leading = values.shape[0]
    grouped = jnp.sum(values.reshape(leading, -1, GSIZE), axis=2)
    return jnp.repeat(grouped, GSIZE, axis=1)


def apply_group_norm(features):
    widened = features.astype(jnp.float32)
    entry_count = features.shape[1] * features.shape[2] * GSIZE
    average = group_average(jnp.sum(widened, axis=(1, 2))) / entry_count
    centred = widened - average[:, None, None, :]
    spread = group_average(jnp.sum(centred * centred, axis=(1, 2))) / entry_count
    inverse_deviation = lax.rsqrt(spread + epsilon)
    return (centred * inverse_deviation[:, None, None, :], inverse_deviation, entry_count)


def spatial_pad(values):
    return jnp.pad(values, ((0, 0), (1, 1), (1, 1), (0, 0)))


def tap_window(padded, tap_index, side_len, flipped):
    row_off, col_off = divmod(tap_index, 3)
    if flipped:
        row_off, col_off = (2 - row_off, 2 - col_off)
    return padded[:, row_off : row_off + side_len, col_off : col_off + side_len, :]


def local(features, weight, group_norm_gain, group_norm_shift, conv_bias, cotangent):
    local_images = features.shape[0]
    side_len = features.shape[1]
    width_in = features.shape[3]
    width_out = cotangent.shape[3]
    images = local_images * lax.axis_size("fsdp") * lax.axis_size("dp")
    normalized_input, inverse_deviation, entry_count = apply_group_norm(features)
    preactivation = normalized_input * group_norm_gain + group_norm_shift
    hidden = jax.nn.silu(preactivation).astype(jnp.bfloat16)
    hidden_pad = spatial_pad(hidden)
    grad_pad = spatial_pad(cotangent)
    full_weight = lax.all_gather(weight, "fsdp", axis=0, tiled=True)
    conv_out = jnp.zeros((local_images, side_len, side_len, width_out), jnp.float32)
    for tap_index in range(9):
        conv_out = conv_out + jnp.einsum(
            "nijc,co->nijo",
            tap_window(hidden_pad, tap_index, side_len, False),
            full_weight[:, tap_index * width_out : (tap_index + 1) * width_out],
            preferred_element_type=jnp.float32,
        )
    output = (conv_out + conv_bias).astype(jnp.bfloat16)
    back_weight = lax.all_gather(weight, "fsdp", axis=0, tiled=True)
    grad_hidden = jnp.zeros((local_images, side_len, side_len, width_in), jnp.float32)
    for tap_index in range(9):
        grad_hidden = grad_hidden + jnp.einsum(
            "nijo,co->nijc",
            tap_window(grad_pad, tap_index, side_len, True),
            back_weight[:, tap_index * width_out : (tap_index + 1) * width_out],
            preferred_element_type=jnp.float32,
        )
    columns = []
    for tap_index in range(9):
        columns.append(
            jnp.einsum(
                "nijc,nijo->co",
                tap_window(hidden_pad, tap_index, side_len, False),
                cotangent,
                preferred_element_type=jnp.float32,
            )
        )
    local_term = jnp.concatenate(columns, axis=1)
    local_term = local_term.reshape(lax.axis_size("fsdp"), -1, 9 * width_out)
    weight_sum = lax.psum_scatter(local_term, "fsdp", scatter_dimension=0)
    weight_total = lax.psum(weight_sum.astype(jnp.float32), "dp")
    weight_grad = weight_total / images
    sigmoid = jax.nn.sigmoid(preactivation)
    preactivation_gradient = grad_hidden * sigmoid * (1.0 + preactivation * (1.0 - sigmoid))
    norm_gradient = preactivation_gradient * group_norm_gain
    first_moment = group_average(jnp.sum(norm_gradient, axis=(1, 2))) / entry_count
    second_moment = (
        group_average(jnp.sum(norm_gradient * normalized_input, axis=(1, 2))) / entry_count
    )
    feature_gradient = (
        (
            norm_gradient
            - first_moment[:, None, None, :]
            - normalized_input * second_moment[:, None, None, :]
        )
        * inverse_deviation[:, None, None, :]
    ).astype(jnp.bfloat16)
    gain_product = jnp.sum(preactivation_gradient * normalized_input, axis=(0, 1, 2))
    shift_term = jnp.sum(preactivation_gradient, axis=(0, 1, 2))
    bias_term = jnp.sum(cotangent.astype(jnp.float32), axis=(0, 1, 2))
    gain_total, shift_total, bias_total = lax.psum(
        (gain_product, shift_term, bias_term), ("fsdp", "dp")
    )
    return (
        output,
        feature_gradient,
        weight_grad,
        gain_total / images,
        shift_total / images,
        bias_total / images,
    )


def solution(mesh):
    in_specs = (
        P(("fsdp", "dp"), None, None, None),
        P("fsdp", None),
        P(),
        P(),
        P(),
        P(("fsdp", "dp"), None, None, None),
    )
    out_specs = (
        P(("fsdp", "dp"), None, None, None),
        P(("fsdp", "dp"), None, None, None),
        P("fsdp", None),
        P(),
        P(),
        P(),
    )
    return jax.shard_map(local, mesh=mesh, in_specs=in_specs, out_specs=out_specs, check_vma=False)
```

profile of v0, /device:TPU:32, one launch (start us, length us, event | category | flops | bytes accessed | tf_op | source)
XLA Modules:
  0.0 481.7 jit_solution(8834222870870780972)
XLA Ops:
  7.2 0.0 all-gather.3.cloned.1.call-start
  7.2 0.7 all-gather.3.cloned.1.call-update
  7.9 0.0 reduce-scatter.4.cloned.1.call-start
  7.9 1.0 convert_reduce_fusion
  9.0 0.1 reshape.235
  9.1 0.1 reduce_sum.100
  9.2 0.1 broadcast_in_dim.8
  9.3 0.1 div.39
  9.4 1.1 fusion.26
  10.4 0.1 reshape.236
  10.5 0.1 reduce_sum.102
  10.7 0.1 broadcast_in_dim.9
  10.7 0.1 rsqrt.14
  10.8 0.0 copy-start
  10.8 105.0 %all-gather.3.cloned.1.call-done = bf16[32,20,5760]{2,1,0:T(8,128)(2,1)} async-done(((bf16[1,20,5760]{2,1,0:T(8,128)(2,1)}), bf16[32,20,5760]{2,1,0:T(8,128)(2,1)}) %all-gather.3.cloned.1.call-update) | async-done | bytes 7372816 | tf_op jit(solution)/shard_map/all_gather | solution.py:48
  115.8 9.2 %reshape.259 = bf16[640,5760]{1,0:T(8,128)(2,1)} reshape(bf16[32,20,5760]{2,1,0:T(8,128)(2,1)} %all-gather.3.cloned.1.call-done) | data formatting | bytes 14745600
  125.0 1.8 fusion.27
  126.8 2.0 convolution_add_fusion.7
  128.8 1.7 convolution_add_fusion.6
  130.5 1.6 convolution_add_fusion.5
  132.1 0.5 convolution_add_fusion.4
  132.6 0.5 convolution_add_fusion.3
  133.1 0.5 convolution_add_fusion.2
  133.5 0.5 convolution_add_fusion.1
  134.0 0.7 fusion.25
  134.7 0.1 reshape.256
  134.8 0.1 reduce_sum.106
  135.0 0.1 broadcast_in_dim.11
  135.0 0.1 div.45
  135.1 0.1 reshape.255
  135.2 0.1 reduce_sum.104
  135.3 0.1 broadcast_in_dim.10
  135.4 0.1 div.43
  135.5 1.1 fusion.24
  136.6 1.6 bitcast_dynamic-update-slice_fusion.8
  138.2 1.6 bitcast_dynamic-update-slice_fusion.7
  139.9 1.6 bitcast_dynamic-update-slice_fusion.6
  141.5 1.7 bitcast_dynamic-update-slice_fusion.5
  143.2 1.6 bitcast_dynamic-update-slice_fusion.4
  144.8 1.7 bitcast_dynamic-update-slice_fusion.3
  146.5 1.6 bitcast_dynamic-update-slice_fusion.2
  148.1 1.7 bitcast_dynamic-update-slice_fusion.1
  149.8 1.6 bitcast_dynamic-update-slice_fusion
  151.4 15.2 %copy.15 = f32[640,5760]{1,0:T(8,128)} copy(f32[640,5760]{0,1:T(8,128)} %bitcast_dynamic-update-slice_fusion) | data formatting | bytes 29491200 | tf_op jit(solution)/shard_map/concatenate | solution.py:77
  166.6 13.2 %reshape.257 = f32[32,20,5760]{2,1,0:T(8,128)} reshape(f32[640,5760]{1,0:T(8,128)} %copy.15) | data formatting | bytes 29491200 | tf_op jit(solution)/shard_map/reshape | solution.py:78
  179.8 0.0 reduce-scatter.4.cloned.1.call-update
  179.8 0.2 all-reduce.6.cloned.1.call-start
  180.1 0.1 convert_reduce_fusion.1
  180.1 1.6 fusion.28
  181.7 1.6 convolution_add_fusion.15
  183.4 1.6 convolution_add_fusion.14
  185.0 1.6 convolution_add_fusion.13
  186.6 1.7 convolution_add_fusion.12
  188.3 1.6 convolution_add_fusion.11
  189.9 1.7 convolution_add_fusion.10
  191.6 1.7 convolution_add_fusion.9
  193.3 197.4 %reduce-scatter.4.cloned.1.call-done = f32[1,20,5760]{2,1,0:T(8,128)} async-done(((f32[32,20,5760]{2,1,0:T(8,128)}), f32[1,20,5760]{2,1,0:T(8,128)}) %reduce-scatter.4.cloned.1.call-update) | async-done | bytes 460816
  390.7 0.0 all-reduce.6.cloned.1.call-update
  390.7 2.3 fusion.5
  393.1 76.2 %all-reduce.3 = (f32[640]{0:T(1024)S(1)}, f32[640]{0:T(1024)S(1)}, f32[640]{0:T(1024)S(1)}) all-reduce(f32[640]{0:T(1024)S(1)} %get-tuple-element.6, f32[640]{0:T(1024)S(1)} %get-tuple-element.9, f32[640]{0:T(1024)S(1)} %convert_reduce_fusion.1), channel_id=1, replica_groups=mesh['fsdp'=32,'dp'=8] {'fsdp','dp'}, use_global_device_ids=true, to_apply=%region_11.12 | all-reduce | flops 1920 | bytes 15360 | tf_op jit(solution)/shard_map/psum | solution.py:100
  469.3 0.6 broadcast_multiply_fusion.3
  469.9 0.6 broadcast_multiply_fusion.1
  470.5 2.8 all-reduce.6.cloned.1.call-done
  473.3 1.9 broadcast_multiply_fusion
  (15 shorter events, 0.1 us)
Async XLA Ops:
  7.2 108.7 %all-gather.3.cloned.1.call-start = ((), (), s32[]{:S(2)}) async-start(), calls=%async_computation.2 | async-start | bytes 9123840 | tf_op jit(solution)/shard_map/all_gather | solution.py:48
  7.9 382.8 %reduce-scatter.4.cloned.1.call-start = ((), (), s32[]{:S(2)}) async-start(), calls=%async_computation.3 | async-start | bytes 18247680
  10.8 114.2 %copy-start = (bf16[1,16,16,640]{3,2,1,0:T(8,128)(2,1)S(1)}, bf16[1,16,16,640]{3,2,1,0:T(8,128)(2,1)}, u32[]{:S(2)}) copy-start(bf16[1,16,16,640]{3,2,1,0:T(8,128)(2,1)} %param.11) | copy-start | bytes 983044
  125.0 7.1 %copy-start.1 = (bf16[640,5760]{1,0:T(8,128)(2,1)S(1)}, bf16[640,5760]{1,0:T(8,128)(2,1)}, u32[]{:S(2)}) copy-start(bf16[640,5760]{1,0:T(8,128)(2,1)} %reshape.259) | copy-start | bytes 22118404
  128.8 5.2 %copy-start.2 = (bf16[1,16,16,640]{3,2,1,0:T(8,128)(2,1)S(1)}, bf16[1,16,16,640]{3,2,1,0:T(8,128)(2,1)}, u32[]{:S(2)}) copy-start(bf16[1,16,16,640]{3,2,1,0:T(8,128)(2,1)} %param.6) | copy-start | bytes 983044
  128.8 5.2 %copy-start.3 = (f32[640]{0:T(1024)S(1)}, f32[640]{0:T(1024)}, u32[]{:S(2)}) copy-start(f32[640]{0:T(1024)} %param.8) | copy-start | bytes 7684
  128.8 5.2 %copy-start.4 = (f32[640]{0:T(1024)S(1)}, f32[640]{0:T(1024)}, u32[]{:S(2)}) copy-start(f32[640]{0:T(1024)} %param.9) | copy-start | bytes 7684
  179.8 293.5 %all-reduce.6.cloned.1.call-start = ((), (), s32[]{:S(2)}) async-start(), calls=%async_computation.1 | async-start | bytes 1105920 | tf_op jit(solution)/shard_map/psum | solution.py:80
  183.4 207.4 %copy-start.5 = (f32[640]{0:T(1024)S(1)}, f32[640]{0:T(1024)}, u32[]{:S(2)}) copy-start(f32[640]{0:T(1024)} %param.10) | copy-start | bytes 7684
Sparse Core Ops, SparseCore 0:
  10.8 105.0 all-gather.2
  180.0 210.6 reduce-scatter.3
  393.4 79.9 all-reduce.5
where the time goes:
time: 483 us; the launch traced here: 482 us
  waiting for transfers between devices  306 us (63%)
  blocking collectives  76.2 us (16%)
  matrix products  39.9 us (8%)
  local copies, waits for them, and re-layouts  38.6 us (8%)
  between operations  14 us (3%)
  other arithmetic  6.84 us (1%)
    unnamed x4, waiting for transfers between devices  198 us
    all_gather x1, waiting for transfers between devices, local(): full_weight = lax.all_gather(weight, 'fsdp', axis=0, tiled=True)  105 us
    psum x1, blocking collectives, local(): lax.psum((gain_product, shift_term, bias_term), ('fsdp', 'dp'))  76.2 us
    dot_general x9, matrix products, local(): jnp.einsum('nijc,co->nijo', tap_window(hidden_pad, tap_index, side_len, F...  15.4 us
    concatenate x1, local copies, waits for them, and re-layouts, local(): local_term = jnp.concatenate(columns, axis=1)  15.2 us
    dot_general x9, matrix products, local(): jnp.einsum('nijc,nijo->co', tap_window(hidden_pad, tap_index, side_len, F...  14.8 us
    reshape x1, local copies, waits for them, and re-layouts, local(): local_term = local_term.reshape(lax.axis_size('fsdp'), -1, 9 * width_out)  13.2 us
  transfers between devices with their start and end apart: 3, of which 3 were waited for; matrix products, arithmetic and copies ran while one was open for 4% of the time, Pallas kernels for 0%

commit v1 on v0

--- a/solution.py
+++ b/solution.py
@@ -45,7 +45,9 @@
     hidden = jax.nn.silu(preactivation).astype(jnp.bfloat16)
     hidden_pad = spatial_pad(hidden)
     grad_pad = spatial_pad(cotangent)
-    full_weight = lax.all_gather(weight, "fsdp", axis=0, tiled=True)
+    full_weight = jnp.concatenate(
+        lax.all_to_all(jnp.stack([weight] * lax.axis_size("fsdp")), "fsdp", 0, 0), axis=0
+    )
     conv_out = jnp.zeros((local_images, side_len, side_len, width_out), jnp.float32)
     for tap_index in range(9):
         conv_out = conv_out + jnp.einsum(

time: 483 us -> 602 us (1.25)
  waiting for transfers between devices: 306 us -> 405 us
  local copies, waits for them, and re-layouts: 38.6 us -> 52.7 us
    all_to_all x0 -> x1, waiting for transfers between devices: none -> 236 us  [local(): lax.all_to_all(jnp.stack([weight] * lax.axis_size('fsdp')), 'fsdp', 0, 0)]
    unnamed x4, waiting for transfers between devices: 198 us -> 61.4 us
    reshape x0 -> x1, local copies, waits for them, and re-layouts: none -> 9.24 us  [local(): jnp.concatenate(lax.all_to_all(jnp.stack([weight] * lax.axis_size('fsdp')...]
  transfers between devices with their start and end apart: 3 -> 4, of which waited for: 3 -> 4; matrix products, arithmetic and copies ran while one was open for 4% -> 5% of each run, Pallas kernels for 0% -> 0%
where the time goes in v1:
time: 602 us; the launch traced here: 600 us
  waiting for transfers between devices  405 us (67%)
  blocking collectives  76.2 us (13%)
  local copies, waits for them, and re-layouts  52.7 us (9%)
  matrix products  39.6 us (7%)
  between operations  14 us (2%)
  other arithmetic  6.84 us (1%)
    all_to_all x1, waiting for transfers between devices, local(): lax.all_to_all(jnp.stack([weight] * lax.axis_size('fsdp')), 'fsdp', 0, 0)  236 us
    all_gather x1, waiting for transfers between devices, local(): back_weight = lax.all_gather(weight, 'fsdp', axis=0, tiled=True)  105 us
    psum x1, blocking collectives, local(): lax.psum((gain_product, shift_term, bias_term), ('fsdp', 'dp'))  76.2 us
    unnamed x4, waiting for transfers between devices  61.4 us
    concatenate x1, local copies, waits for them, and re-layouts, local(): local_term = jnp.concatenate(columns, axis=1)  15.2 us
    dot_general x9, matrix products, local(): jnp.einsum('nijc,co->nijo', tap_window(hidden_pad, tap_index, side_len, F...  15.2 us
    dot_general x9, matrix products, local(): jnp.einsum('nijc,nijo->co', tap_window(hidden_pad, tap_index, side_len, F...  14.8 us
    reshape x1, local copies, waits for them, and re-layouts, local(): local_term = local_term.reshape(lax.axis_size('fsdp'), -1, 9 * width_out)  13.2 us
  transfers between devices with their start and end apart: 4, of which 4 were waited for; matrix products, arithmetic and copies ran while one was open for 5% of the time, Pallas kernels for 0%

profile of v1, /device:TPU:32, one launch (start us, length us, event | category | flops | bytes accessed | tf_op | source)
XLA Modules:
  0.0 600.3 jit_solution(9881854161160671474)
XLA Ops:
  7.2 0.7 all-gather.3.cloned.1.call-update
  7.9 1.0 convert_reduce_fusion
  9.0 0.1 reshape.240
  9.1 0.1 reduce_sum.100
  9.2 0.1 broadcast_in_dim.8
  9.3 0.1 div.39
  9.4 1.1 fusion.28
  10.4 0.1 reshape.241
  10.5 0.1 reduce_sum.102
  10.7 0.1 broadcast_in_dim.9
  10.7 0.1 rsqrt.14
  10.8 105.0 %all-gather.3.cloned.1.call-done = bf16[32,20,5760]{2,1,0:T(8,128)(2,1)} async-done(((bf16[1,20,5760]{2,1,0:T(8,128)(2,1)}), bf16[32,20,5760]{2,1,0:T(8,128)(2,1)}) %all-gather.3.cloned.1.call-update) | async-done | bytes 7372816 | tf_op jit(solution)/shard_map/all_gather | solution.py:60
  115.8 9.2 %reshape.265 = bf16[640,5760]{1,0:T(8,128)(2,1)} reshape(bf16[32,20,5760]{2,1,0:T(8,128)(2,1)} %all-gather.3.cloned.1.call-done) | data formatting | bytes 14745600
  125.1 1.8 fusion.6
  126.8 2.0 convolution_add_fusion.7
  128.9 1.6 convolution_add_fusion.6
  130.5 1.6 convolution_add_fusion.5
  132.2 0.5 convolution_add_fusion.4
  132.6 0.5 convolution_add_fusion.3
  133.1 0.5 convolution_add_fusion.2
  133.6 0.5 convolution_add_fusion.1
  134.1 0.7 fusion.27
  134.8 0.1 reshape.262
  134.9 0.1 reduce_sum.106
  135.0 0.1 broadcast_in_dim.11
  135.1 0.1 div.45
  135.2 0.1 reshape.261
  135.2 0.1 reduce_sum.104
  135.4 0.1 broadcast_in_dim.10
  135.4 0.1 div.43
  135.5 1.1 fusion.26
  136.6 1.6 bitcast_dynamic-update-slice_fusion.8
  138.3 1.6 bitcast_dynamic-update-slice_fusion.7
  139.9 1.6 bitcast_dynamic-update-slice_fusion.6
  141.5 1.7 bitcast_dynamic-update-slice_fusion.5
  143.2 1.6 bitcast_dynamic-update-slice_fusion.4
  144.8 1.7 bitcast_dynamic-update-slice_fusion.3
  146.5 1.6 bitcast_dynamic-update-slice_fusion.2
  148.2 1.7 bitcast_dynamic-update-slice_fusion.1
  149.8 1.6 bitcast_dynamic-update-slice_fusion
  151.5 15.2 %copy.15 = f32[640,5760]{1,0:T(8,128)} copy(f32[640,5760]{0,1:T(8,128)} %bitcast_dynamic-update-slice_fusion) | data formatting | bytes 29491200 | tf_op jit(solution)/shard_map/concatenate | solution.py:79
  166.6 13.2 %reshape.263 = f32[32,20,5760]{2,1,0:T(8,128)} reshape(f32[640,5760]{1,0:T(8,128)} %copy.15) | data formatting | bytes 29491200 | tf_op jit(solution)/shard_map/reshape | solution.py:80
  179.9 0.9 copy-done.3
  180.8 3.9 stack.2
  184.7 5.2 all-to-all-start
  190.0 0.2 all-reduce.6.cloned.1.call-start
  190.2 0.1 convert_reduce_fusion.1
  190.3 236.5 %all-to-all-done = bf16[32,20,5760]{2,1,0:T(8,128)(2,1)} async-done(((bf16[32,20,5760]{2,1,0:T(8,128)(2,1)}), bf16[32,20,5760]{2,1,0:T(8,128)(2,1)}, u32[]{:S(2)}, u32[]{:S(2)}) %all-to-all-start) | async-done | bytes 7372832 | tf_op jit(solution)/shard_map/all_to_all | solution.py:49
  426.8 9.2 %reshape.243 = bf16[640,5760]{1,0:T(8,128)(2,1)} reshape(bf16[32,20,5760]{2,1,0:T(8,128)(2,1)} %all-to-all-done) | data formatting | bytes 14745600 | tf_op jit(solution)/shard_map/reshape | solution.py:48
  436.0 1.6 fusion.7
  437.6 1.6 convolution_add_fusion.15
  439.2 1.6 convolution_add_fusion.14
  440.9 1.6 convolution_add_fusion.13
  442.5 1.6 convolution_add_fusion.12
  444.1 1.6 convolution_add_fusion.11
  445.7 1.6 convolution_add_fusion.10
  447.3 1.6 convolution_add_fusion.9
  448.9 60.7 %reduce-scatter.4.cloned.1.call-done = f32[1,20,5760]{2,1,0:T(8,128)} async-done(((f32[32,20,5760]{2,1,0:T(8,128)}), f32[1,20,5760]{2,1,0:T(8,128)}) %reduce-scatter.4.cloned.1.call-update) | async-done | bytes 460816
  509.6 2.3 fusion.5
  511.9 76.2 %all-reduce.3 = (f32[640]{0:T(1024)S(1)}, f32[640]{0:T(1024)S(1)}, f32[640]{0:T(1024)S(1)}) all-reduce(f32[640]{0:T(1024)S(1)} %get-tuple-element.6, f32[640]{0:T(1024)S(1)} %get-tuple-element.9, f32[640]{0:T(1024)S(1)} %convert_reduce_fusion.1), channel_id=1, replica_groups=mesh['fsdp'=32,'dp'=8] {'fsdp','dp'}, use_global_device_ids=true, to_apply=%region_11.12 | all-reduce | flops 1920 | bytes 15360 | tf_op jit(solution)/shard_map/psum | solution.py:102
  588.2 0.6 broadcast_multiply_fusion.3
  588.8 0.6 broadcast_multiply_fusion.1
  589.4 2.5 all-reduce.6.cloned.1.call-done
  591.9 1.9 broadcast_multiply_fusion
  (21 shorter events, 0.2 us)
Async XLA Ops:
  7.2 108.7 %all-gather.3.cloned.1.call-start = ((), (), s32[]{:S(2)}) async-start(), calls=%async_computation.3 | async-start | bytes 9123840 | tf_op jit(solution)/shard_map/all_gather | solution.py:60
  7.9 501.7 %reduce-scatter.4.cloned.1.call-start = ((), (), s32[]{:S(2)}) async-start(), calls=%async_computation.4 | async-start | bytes 18247680
  10.8 114.2 %copy-start = (bf16[1,16,16,640]{3,2,1,0:T(8,128)(2,1)S(1)}, bf16[1,16,16,640]{3,2,1,0:T(8,128)(2,1)}, u32[]{:S(2)}) copy-start(bf16[1,16,16,640]{3,2,1,0:T(8,128)(2,1)} %param.11) | copy-start | bytes 983044
  125.1 7.1 %copy-start.1 = (bf16[640,5760]{1,0:T(8,128)(2,1)S(1)}, bf16[640,5760]{1,0:T(8,128)(2,1)}, u32[]{:S(2)}) copy-start(bf16[640,5760]{1,0:T(8,128)(2,1)} %reshape.265) | copy-start | bytes 22118404
  128.8 5.2 copy-start.2
  128.8 5.2 copy-start.4
  128.9 5.2 copy-start.5
  179.8 1.0 copy-start.3
  184.7 242.0 %all-to-all-start = ((bf16[32,20,5760]{2,1,0:T(8,128)(2,1)}), bf16[32,20,5760]{2,1,0:T(8,128)(2,1)}, u32[]{:S(2)}, u32[]{:S(2)}) async-start(bf16[32,20,5760]{2,1,0:T(8,128)(2,1)} %stack.2), calls=%async_computation | async-start | bytes 17694720 | tf_op jit(solution)/shard_map/all_to_all | solution.py:49
  190.0 401.9 %all-reduce.6.cloned.1.call-start = ((), (), s32[]{:S(2)}) async-start(), calls=%async_computation.2 | async-start | bytes 1105920 | tf_op jit(solution)/shard_map/psum | solution.py:82
  439.2 70.4 %copy-start.6 = (f32[640]{0:T(1024)S(1)}, f32[640]{0:T(1024)}, u32[]{:S(2)}) copy-start(f32[640]{0:T(1024)} %param.10) | copy-start | bytes 7684
Sparse Core Ops, SparseCore 0:
  10.8 105.0 all-gather.2
  180.0 329.5 reduce-scatter.3
  512.2 79.6 all-reduce.5
